TPU v7x, 512 devices: a whole 4x8x8 slice. The times are simulated.
512 devices in a mesh: dp: 32 (over x, y_hi, core), fsdp: 16 (over y_lo, z).
Axes of the slice: x: 4, y: 8 (y_hi: 4, y_lo: 2; y = y_hi * 2 + y_lo), z: 8, core: 2. Of those that a mesh axis runs over, the one named last changes fastest.
Arguments:
- hidden: bfloat16 [4, 2048, 16, 4096], P(None, 'dp', 'fsdp'), may hold values from -6 to 6
- frozen_query_rows: bfloat16 [4, 2048, 16, 2048], P(None, 'dp', 'fsdp'), may hold values from -10 to 10
- output_gradient: bfloat16 [4, 2048, 16, 2048], P(None, 'dp', 'fsdp'), may hold values from -6 to 6
- token_log_ratio: float32 [4, 2048, 16], P(None, 'dp', 'fsdp'), may hold values from -0.15625 to 0.15625
- lengths: int32 [4], replicated, may hold values from 1 to 32768, as said below
- response_win_probability: float32 [4], replicated, may hold values from 0.05 to 0.95
- cached_prompt_keys: bfloat16 [1024, 512], P('fsdp'), may hold values from -7.5 to 7.5
- cached_prompt_values: bfloat16 [1024, 512], P('fsdp'), may hold values from -6 to 6
- adapter_down_factor: bfloat16 [4096, 64], P('fsdp'), may hold values from -0.09375 to 0.09375
- adapter_up_factor: bfloat16 [64, 2048], P(None, 'fsdp'), may hold values from -0.125 to 0.125
- attention_norm_gain: bfloat16 [4096], P('fsdp'), may hold values from 0.5 to 1.5
Outputs:
- grad_down: float32 [4096, 64], P('fsdp')
- grad_up: float32 [64, 2048], P(None, 'fsdp')
- seq_ratio: float32 [4], replicated
Inputs may be any that keep to these rules, and one draw needn't show every extreme that they name: The lengths sum to 65472 and the longest is exactly 32768.
All inputs are finite; a program needn't handle non-finite values.
Results may differ from a plain program's by a relative error of at most 0.012.
Values may be sent and summed in bfloat16 or wider, within the bound.
A program may use at most 128 MiB of HBM per device.

v0:
```python
import math
import jax
import jax.numpy as jnp
from jax import lax
from jax.sharding import PartitionSpec as P

HEAD_SIZE = 128
QUERY_HEADS = 16
KEY_VALUE_HEADS = 4
target_scale = 1.0
norm_epsilon = 1e-05


def attend(query_vectors, cotangent, key_rows, value_rows):
    row_count = query_vectors.shape[0]
    queries_per_group = QUERY_HEADS // KEY_VALUE_HEADS
    score_scale = 1.0 / math.sqrt(HEAD_SIZE)
    pieces = []
    for shared_key_head in range(KEY_VALUE_HEADS):
        head_start = shared_key_head * queries_per_group * HEAD_SIZE
        head_stop = head_start + queries_per_group * HEAD_SIZE
        head_query = query_vectors[:, head_start:head_stop].reshape(
            row_count, queries_per_group, HEAD_SIZE
        )
        head_grad = cotangent[:, head_start:head_stop].reshape(
            row_count, queries_per_group, HEAD_SIZE
        )
        head_key = key_rows[:, shared_key_head * HEAD_SIZE : (shared_key_head + 1) * HEAD_SIZE]
        head_value = value_rows[:, shared_key_head * HEAD_SIZE : (shared_key_head + 1) * HEAD_SIZE]
        scores = (
            jnp.einsum("nhd,jd->nhj", head_query, head_key, preferred_element_type=jnp.float32)
            * score_scale
        )
        row_top = jnp.max(scores, axis=2, keepdims=True)
        exponent = jnp.exp(scores - row_top)
        row_total = jnp.sum(exponent, axis=2, keepdims=True)
        weights = exponent.astype(jnp.bfloat16)
        mixed_out = (
            jnp.einsum("nhj,jd->nhd", weights, head_value, preferred_element_type=jnp.float32)
            / row_total
        )
        inner_prod = jnp.sum(head_grad.astype(jnp.float32) * mixed_out, axis=2, keepdims=True)
        grad_prob = jnp.einsum(
            "nhd,jd->nhj", head_grad, head_value, preferred_element_type=jnp.float32
        )
        grad_score = (weights.astype(jnp.float32) / row_total * (grad_prob - inner_prod)).astype(
            jnp.bfloat16
        )
        query_gradient = (
            jnp.einsum("nhj,jd->nhd", grad_score, head_key, preferred_element_type=jnp.float32)
            * score_scale
        )
        pieces.append(query_gradient.reshape(row_count, queries_per_group * HEAD_SIZE))
    return jnp.concatenate(pieces, axis=1).astype(jnp.bfloat16)


def body(
    hidden,
    frozen_query_rows,
    output_gradient,
    token_log_ratio,
    lengths,
    response_win_probability,
    cached_prompt_keys,
    cached_prompt_values,
    adapter_down_factor,
    adapter_up_factor,
    attention_norm_gain,
):
    fsdp_count = lax.axis_size("fsdp")
    dp_index = lax.axis_index("dp")
    fsdp_index = lax.axis_index("fsdp")
    responses, per_device, single, feature_count = hidden.shape
    home_rows = responses * per_device
    local_rows = jnp.arange(per_device, dtype=jnp.int32)
    position = (dp_index * per_device + local_rows) * fsdp_count + fsdp_index
    is_valid = position[None, :] < lengths[:, None]
    partial_value = jnp.sum(jnp.where(is_valid, token_log_ratio[:, :, 0], 0.0), axis=1)
    seq_ratio = lax.psum(partial_value, ("dp", "fsdp"))
    weighting = 2.0 * (seq_ratio - target_scale * (response_win_probability - 0.5)) / responses
    down_full, up_full, gain_full = (
        lax.all_gather(adapter_down_factor, "fsdp", axis=0, tiled=True),
        lax.all_gather(adapter_up_factor, "fsdp", axis=1, tiled=True),
        lax.all_gather(attention_norm_gain, "fsdp", axis=0, tiled=True),
    )
    key_rows, value_rows = (
        lax.all_gather(cached_prompt_keys, "fsdp", axis=0, tiled=True),
        lax.all_gather(cached_prompt_values, "fsdp", axis=0, tiled=True),
    )
    widened = hidden.reshape(home_rows, feature_count).astype(jnp.float32)
    inverse = lax.rsqrt(jnp.mean(widened * widened, axis=1, keepdims=True) + norm_epsilon)
    normed_input = (widened * inverse * gain_full.astype(jnp.float32)).astype(jnp.bfloat16)
    lowrank_hidden = jnp.dot(normed_input, down_full, preferred_element_type=jnp.float32).astype(
        jnp.bfloat16
    )
    row_mask = is_valid.reshape(home_rows)
    row_coef = jnp.repeat(weighting, per_device)
    base_rows = frozen_query_rows.reshape(home_rows, -1)
    cotangent = jnp.where(
        row_mask[:, None],
        row_coef[:, None] * output_gradient.reshape(home_rows, -1).astype(jnp.float32),
        0.0,
    ).astype(jnp.bfloat16)
    query_vectors = (
        base_rows.astype(jnp.float32)
        + jnp.dot(lowrank_hidden, up_full, preferred_element_type=jnp.float32)
    ).astype(jnp.bfloat16)
    query_gradient = attend(query_vectors, cotangent, key_rows, value_rows)
    up_term = jnp.dot(lowrank_hidden.T, query_gradient, preferred_element_type=jnp.float32)
    gradient_lowrank = jnp.dot(
        query_gradient, up_full.T, preferred_element_type=jnp.float32
    ).astype(jnp.bfloat16)
    down_term = jnp.dot(normed_input.T, gradient_lowrank, preferred_element_type=jnp.float32)
    down_sum, up_sum = lax.psum((down_term, up_term), ("dp", "fsdp"))
    down_factor_part = adapter_down_factor.shape[0]
    up_factor_part = adapter_up_factor.shape[1]
    grad_down = lax.dynamic_slice_in_dim(
        down_sum, fsdp_index * down_factor_part, down_factor_part, 0
    )
    grad_up = lax.dynamic_slice_in_dim(up_sum, fsdp_index * up_factor_part, up_factor_part, 1)
    return (grad_down, grad_up, seq_ratio)


def solution(mesh):
    in_specs = (
        P(None, "dp", "fsdp", None),
        P(None, "dp", "fsdp", None),
        P(None, "dp", "fsdp", None),
        P(None, "dp", "fsdp"),
        P(),
        P(),
        P("fsdp", None),
        P("fsdp", None),
        P("fsdp", None),
        P(None, "fsdp"),
        P("fsdp"),
    )
    out_specs = (P("fsdp", None), P(None, "fsdp"), P())
    return jax.shard_map(body, mesh=mesh, in_specs=in_specs, out_specs=out_specs, check_vma=False)
```

profile of v0, /device:TPU:17, one launch (start us, length us, event | category | flops | bytes accessed | tf_op | source)
XLA Modules:
  0.0 574.0 jit_solution(2248930495816452318)
XLA Ops:
  7.2 0.7 all-gather.4.cloned.1.call-update
  8.0 0.7 all-gather.6.cloned.1.call-update
  8.7 0.9 select_reduce_fusion
  9.6 105.0 %psum.21 = f32[4]{0:T(128)S(1)} all-reduce(f32[4]{0:T(128)S(1)} %get-tuple-element.5), channel_id=1, replica_groups=mesh['dp'=32,'fsdp'=16] {'dp','fsdp'}, use_global_device_ids=true, to_apply=%region_4.5 | all-reduce | flops 4 | bytes 32 | tf_op jit(solution)/shard_map/psum | solution.py:79
  116.1 2.1 multiply_reduce_fusion
  118.3 24.8 %all-gather = bf16[16,1,256]{2,1,0:T(2,128)(2,1)S(1)} all-gather(bf16[1,1,256]{2,1,0:T(2,128)(2,1)S(1)} %reshape.122), channel_id=1, replica_groups=mesh['dp'=32,'fsdp'=16] {'fsdp'}, dimensions={0}, use_global_device_ids=true | all-gather | bytes 8704 | tf_op jit(solution)/shard_map/all_gather | solution.py:84
  143.1 2.2 fusion.1
  145.7 1.3 slice_bitcast_fusion.35
  147.0 1.7 reshape.117
  148.7 1.7 reshape.114
  150.5 1.7 reshape.111
  152.2 0.8 reshape.108
  152.9 24.4 %all_gather.17 = bf16[64,2048]{1,0:T(8,128)(2,1)S(1)} all-gather(bf16[64,128]{1,0:T(8,128)(2,1)S(1)} %copy-done.17), channel_id=1, replica_groups=mesh['dp'=32,'fsdp'=16] {'fsdp'}, dimensions={1}, use_global_device_ids=true | all-gather | bytes 278528 | tf_op jit(solution)/shard_map/all_gather | solution.py:83
  177.3 27.5 %all_gather.16 = bf16[4096,64]{0,1:T(8,128)(2,1)S(1)} all-gather(bf16[256,64]{0,1:T(8,128)(2,1)S(1)} %copy-done.16), channel_id=1, replica_groups=mesh['dp'=32,'fsdp'=16] {'fsdp'}, dimensions={0}, use_global_device_ids=true | all-gather | bytes 557056 | tf_op jit(solution)/shard_map/all_gather | solution.py:82
  204.8 0.8 convolution_convert_fusion.1
  206.2 0.9 slice_bitcast_fusion.11
  207.1 1.7 multiply_reduce_fusion.4
  208.8 2.0 copy-done
  210.8 0.9 fusion.2
  211.9 3.0 fusion.39
  215.0 0.8 fusion.26
  216.4 1.9 multiply_reduce_fusion.1
  218.3 1.9 copy-done.1
  220.3 0.9 fusion.8
  221.2 0.8 copy.39
  222.0 3.1 fusion.30
  225.1 0.8 fusion.29
  226.6 1.8 multiply_reduce_fusion.2
  228.4 2.0 copy-done.2
  230.3 0.9 fusion.6
  231.3 0.8 copy.35
  232.1 3.1 fusion.33
  235.2 0.8 fusion.28
  236.6 1.8 multiply_reduce_fusion.3
  238.4 1.9 copy-done.3
  240.4 1.1 fusion.4
  241.5 0.8 copy.31
  242.3 3.1 fusion.36
  245.4 0.8 fusion.27
  246.9 4.8 fusion.21
  251.7 4.8 fusion.24
  256.5 4.8 fusion.23
  261.3 4.8 fusion.22
  266.2 3.6 fusion.25
  269.8 2.2 fusion.70
  272.0 292.6 %all-reduce.3.cloned.1.call-done = (f32[4096,64]{0,1:T(8,128)}, f32[64,2048]{1,0:T(8,128)}) async-done(((f32[4096,64]{0,1:T(8,128)}, f32[64,2048]{1,0:T(8,128)}), (f32[4096,64]{0,1:T(8,128)}, f32[64,2048]{1,0:T(8,128)})) %all-reduce.3.cloned.1.call-update) | async-done | bytes 1572880 | tf_op jit(solution)/shard_map/psum | solution.py:114
  564.6 1.5 constant_dynamic-slice_fusion.1
  566.1 1.4 constant_dynamic-slice_fusion
  (82 shorter events, 5.7 us)
Async XLA Ops:
  7.2 138.2 %copy-start.6 = (bf16[4,64,1,2048]{3,1,2,0:T(8,128)(2,1)S(1)}, bf16[4,64,1,2048]{3,1,2,0:T(8,128)(2,1)}, u32[]{:S(2)}) copy-start(bf16[4,64,1,2048]{3,1,2,0:T(8,128)(2,1)} %param.13) | copy-start | bytes 3145732
  7.2 199.9 %all-gather.4.cloned.1.call-start = ((), (), s32[]{:S(2)}) async-start(), calls=%async_computation | async-start | bytes 1114112 | tf_op jit(solution)/shard_map/all_gather | solution.py:87
  7.9 204.0 %all-gather.6.cloned.1.call-start = ((), (), s32[]{:S(2)}) async-start(), calls=%async_computation.1 | async-start | bytes 1114112 | tf_op jit(solution)/shard_map/all_gather | solution.py:88
  8.7 555.9 %all-reduce.3.cloned.1.call-start = ((), (), s32[]{:S(2)}) async-start(), calls=%async_computation.2 | async-start | bytes 3145728 | tf_op jit(solution)/shard_map/psum | solution.py:114
  114.6 3.7 copy-start.31
  145.3 7.6 %copy-start.17 = (bf16[64,128]{1,0:T(8,128)(2,1)S(1)}, bf16[64,128]{1,0:T(8,128)(2,1)}, u32[]{:S(2)}) copy-start(bf16[64,128]{1,0:T(8,128)(2,1)} %param.20) | copy-start | bytes 49156
  145.4 32.0 %copy-start.16 = (bf16[256,64]{0,1:T(8,128)(2,1)S(1)}, bf16[256,64]{0,1:T(8,128)(2,1)}, u32[]{:S(2)}) copy-start(bf16[256,64]{0,1:T(8,128)(2,1)} %param.19) | copy-start | bytes 98308
  145.7 59.9 %copy-start.5 = (bf16[4,64,1,2048]{3,1,2,0:T(8,128)(2,1)S(1)}, bf16[4,64,1,2048]{3,1,2,0:T(8,128)(2,1)}, u32[]{:S(2)}) copy-start(bf16[4,64,1,2048]{3,1,2,0:T(8,128)(2,1)} %param.12) | copy-start | bytes 3145732
  205.6 0.6 copy-start.14
  208.8 2.0 copy-start
  210.8 4.2 copy-start.10
  211.7 6.6 %copy-start.18 = (f32[256,4]{0,1:T(4,128)}, f32[256,4]{0,1:T(4,128)S(1)}, u32[]{:S(2)}) copy-start(f32[256,4]{0,1:T(4,128)S(1)} %fusion.2) | copy-start | bytes 12292
  216.4 5.6 copy-start.4
  218.3 1.9 copy-start.1
  221.2 0.8 copy-start.19
  222.0 3.1 copy-start.9
  222.0 3.1 copy-start.11
  228.4 2.0 copy-start.2
  231.3 0.8 copy-start.21
  232.1 3.1 copy-start.8
  232.1 3.1 copy-start.12
  238.4 1.9 copy-start.3
  241.5 0.8 copy-start.23
  242.3 3.1 copy-start.7
  242.3 3.1 copy-start.13
  246.9 4.8 copy-start.20
  246.9 4.8 copy-start.25
  251.7 4.8 copy-start.22
  251.7 4.8 copy-start.26
  256.5 4.8 copy-start.24
  256.5 4.8 copy-start.27
  266.2 3.7 copy-start.15
  266.2 3.7 copy-start.28
  266.2 3.7 copy-start.29
  266.2 3.7 copy-start.30
Sparse Core Ops, SparseCore 0:
  10.1 66.9 all-gather.3
  79.2 69.6 all-gather.5
  272.2 292.3 all-reduce.2
where the time goes:
time: 575 us; the launch traced here: 574 us
  waiting for transfers between devices  294 us (51%)
  blocking collectives  182 us (32%)
  matrix products  45.8 us (8%)
  local copies, waits for them, and re-layouts  25.3 us (4%)
  between operations  14.1 us (2%)
  other arithmetic  13.1 us (2%)
    psum x1, waiting for transfers between devices, body(): down_sum, up_sum = lax.psum((down_term, up_term), ('dp', 'fsdp'))  293 us
    psum x1, blocking collectives, body(): seq_ratio = lax.psum(partial_value, ('dp', 'fsdp'))  105 us
    all_gather x1, blocking collectives, body(): lax.all_gather(adapter_down_factor, 'fsdp', axis=0, tiled=True)  27.5 us
    all_gather x1, blocking collectives, body(): lax.all_gather(attention_norm_gain, 'fsdp', axis=0, tiled=True)  24.8 us
    all_gather x1, blocking collectives, body(): lax.all_gather(adapter_up_factor, 'fsdp', axis=1, tiled=True)  24.4 us
    dot_general x4, matrix products, attend(): jnp.einsum('nhj,jd->nhd', grad_score, head_key, preferred_element_type=jn...  19.2 us
    dot_general x4, matrix products, attend(): jnp.einsum('nhj,jd->nhd', weights, head_value, preferred_element_type=jnp...  12.3 us
  transfers between devices with their start and end apart: 3, of which 1 were waited for; matrix products, arithmetic and copies ran while one was open for 3% of the time, Pallas kernels for 0%

commit v1 on v0

--- a/solution.py
+++ b/solution.py
@@ -9,6 +9,11 @@
 KEY_VALUE_HEADS = 4
 target_scale = 1.0
 norm_epsilon = 1e-05
+
+
+def by_each_axis(array, inner_axis, outer_axis):
+    inner = lax.psum(array, inner_axis)
+    return lax.psum(inner, outer_axis)
 
 
 def attend(query_vectors, cotangent, key_rows, value_rows):
@@ -111,7 +116,7 @@
         query_gradient, up_full.T, preferred_element_type=jnp.float32
     ).astype(jnp.bfloat16)
     down_term = jnp.dot(normed_input.T, gradient_lowrank, preferred_element_type=jnp.float32)
-    down_sum, up_sum = lax.psum((down_term, up_term), ("dp", "fsdp"))
+    down_sum, up_sum = by_each_axis((down_term, up_term), "dp", "fsdp")
     down_factor_part = adapter_down_factor.shape[0]
     up_factor_part = adapter_up_factor.shape[1]
     grad_down = lax.dynamic_slice_in_dim(

time: 575 us -> 738 us (1.28)
  the two profiles are of different devices: /device:TPU:17 before, /device:TPU:2 now
where the time goes in v1:
time: 738 us
  waiting for transfers between devices  435 us (59%)
  blocking collectives  204 us (28%)
  matrix products  45.8 us (6%)
  local copies, waits for them, and re-layouts  25.2 us (3%)
  between operations  14.1 us (2%)
  other arithmetic  13.1 us (2%)
    psum x1, waiting for transfers between devices, by_each_axis(): inner = lax.psum(array, inner_axis)  273 us
    psum x1, waiting for transfers between devices, by_each_axis(): return lax.psum(inner, outer_axis)  161 us
    psum x1, blocking collectives, body(): seq_ratio = lax.psum(partial_value, ('dp', 'fsdp'))  107 us
    all_gather x1, blocking collectives, body(): lax.all_gather(adapter_down_factor, 'fsdp', axis=0, tiled=True)  34 us
    all_gather x1, blocking collectives, body(): lax.all_gather(adapter_up_factor, 'fsdp', axis=1, tiled=True)  31.7 us
    all_gather x1, blocking collectives, body(): lax.all_gather(attention_norm_gain, 'fsdp', axis=0, tiled=True)  30.7 us
    dot_general x4, matrix products, attend(): jnp.einsum('nhj,jd->nhd', grad_score, head_key, preferred_element_type=jn...  19.2 us
  transfers between devices with their start and end apart: 4, of which 2 were waited for; matrix products, arithmetic and copies ran while one was open for 3% of the time, Pallas kernels for 0%

profile of v1, /device:TPU:2, one launch (start us, length us, event | category | flops | bytes accessed | tf_op | source)
XLA Modules:
  0.0 737.6 jit_solution(1639249956733935230)
XLA Ops:
  8.0 0.7 all-gather.6.cloned.1.call-update
  8.7 0.9 select_reduce_fusion
  9.6 107.3 %psum.35 = f32[4]{0:T(128)S(1)} all-reduce(f32[4]{0:T(128)S(1)} %get-tuple-element.7), channel_id=1, replica_groups=mesh['dp'=32,'fsdp'=16] {'dp','fsdp'}, use_global_device_ids=true, to_apply=%region_4.5 | all-reduce | flops 4 | bytes 32 | tf_op jit(solution)/shard_map/psum | solution.py:84
  118.4 2.1 multiply_reduce_fusion
  120.6 30.7 %all-gather = bf16[16,1,256]{2,1,0:T(2,128)(2,1)S(1)} all-gather(bf16[1,1,256]{2,1,0:T(2,128)(2,1)S(1)} %reshape.122), channel_id=1, replica_groups=mesh['dp'=32,'fsdp'=16] {'fsdp'}, dimensions={0}, use_global_device_ids=true | all-gather | bytes 8704 | tf_op jit(solution)/shard_map/all_gather | solution.py:89
  151.4 2.2 fusion.1
  154.0 1.3 slice_bitcast_fusion.35
  155.3 1.7 reshape.117
  157.0 1.7 reshape.114
  158.8 1.7 reshape.111
  160.5 0.8 reshape.108
  161.2 31.7 %all_gather.17 = bf16[64,2048]{1,0:T(8,128)(2,1)S(1)} all-gather(bf16[64,128]{1,0:T(8,128)(2,1)S(1)} %copy-done.17), channel_id=1, replica_groups=mesh['dp'=32,'fsdp'=16] {'fsdp'}, dimensions={1}, use_global_device_ids=true | all-gather | bytes 278528 | tf_op jit(solution)/shard_map/all_gather | solution.py:88
  192.9 34.0 %all_gather.16 = bf16[4096,64]{0,1:T(8,128)(2,1)S(1)} all-gather(bf16[256,64]{0,1:T(8,128)(2,1)S(1)} %copy-done.16), channel_id=1, replica_groups=mesh['dp'=32,'fsdp'=16] {'fsdp'}, dimensions={0}, use_global_device_ids=true | all-gather | bytes 557056 | tf_op jit(solution)/shard_map/all_gather | solution.py:87
  226.9 0.8 convolution_convert_fusion.1
  228.3 0.9 slice_bitcast_fusion.11
  229.2 1.7 multiply_reduce_fusion.4
  231.0 2.0 copy-done
  233.0 0.9 fusion.2
  234.1 3.0 fusion.39
  237.1 0.8 fusion.26
  238.6 1.9 multiply_reduce_fusion.1
  240.5 1.9 copy-done.1
  242.4 0.9 fusion.8
  243.3 0.8 copy.39
  244.1 3.1 fusion.30
  247.2 0.8 fusion.29
  248.7 1.8 multiply_reduce_fusion.2
  250.5 1.9 copy-done.2
  252.4 0.9 fusion.6
  253.4 0.8 copy.35
  254.2 3.1 fusion.33
  257.3 0.8 fusion.28
  258.7 1.8 multiply_reduce_fusion.3
  260.5 1.9 copy-done.3
  262.5 1.1 fusion.4
  263.6 0.8 copy.31
  264.4 3.1 fusion.36
  267.5 0.8 fusion.27
  269.0 4.8 fusion.21
  273.8 4.8 fusion.24
  278.6 4.8 fusion.23
  283.4 4.8 fusion.22
  288.3 3.6 fusion.25
  291.9 2.2 fusion.70
  294.2 272.8 %all-reduce.5.cloned.1.call-done = (f32[4096,64]{0,1:T(8,128)}, f32[64,2048]{1,0:T(8,128)}) async-done(((f32[4096,64]{0,1:T(8,128)}, f32[64,2048]{1,0:T(8,128)}), (f32[4096,64]{0,1:T(8,128)}, f32[64,2048]{1,0:T(8,128)})) %all-reduce.5.cloned.1.call-update) | async-done | bytes 1572880 | tf_op jit(solution)/shard_map/psum | solution.py:15
  567.1 161.1 %all-reduce.7.cloned.1.call-done = (f32[4096,64]{0,1:T(8,128)}, f32[64,2048]{1,0:T(8,128)}) async-done(((f32[4096,64]{0,1:T(8,128)}, f32[64,2048]{1,0:T(8,128)}), (f32[4096,64]{0,1:T(8,128)}, f32[64,2048]{1,0:T(8,128)})) %all-reduce.7.cloned.1.call-update) | async-done | bytes 1572880 | tf_op jit(solution)/shard_map/psum | solution.py:16
  728.2 1.5 constant_dynamic-slice_fusion.1
  729.7 1.4 constant_dynamic-slice_fusion
  (85 shorter events, 6.4 us)
Async XLA Ops:
  7.2 146.5 %copy-start.6 = (bf16[4,64,1,2048]{3,1,2,0:T(8,128)(2,1)S(1)}, bf16[4,64,1,2048]{3,1,2,0:T(8,128)(2,1)}, u32[]{:S(2)}) copy-start(bf16[4,64,1,2048]{3,1,2,0:T(8,128)(2,1)} %param.13) | copy-start | bytes 3145732
  7.2 222.1 %all-gather.4.cloned.1.call-start = ((), (), s32[]{:S(2)}) async-start(), calls=%async_computation | async-start | bytes 1114112 | tf_op jit(solution)/shard_map/all_gather | solution.py:92
  7.9 226.1 %all-gather.6.cloned.1.call-start = ((), (), s32[]{:S(2)}) async-start(), calls=%async_computation.1 | async-start | bytes 1114112 | tf_op jit(solution)/shard_map/all_gather | solution.py:93
  8.7 558.4 %all-reduce.5.cloned.1.call-start = ((), (), s32[]{:S(2)}) async-start(), calls=%async_computation.2 | async-start | bytes 3145728 | tf_op jit(solution)/shard_map/psum | solution.py:15
  116.9 3.7 copy-start.31
  153.6 7.6 %copy-start.17 = (bf16[64,128]{1,0:T(8,128)(2,1)S(1)}, bf16[64,128]{1,0:T(8,128)(2,1)}, u32[]{:S(2)}) copy-start(bf16[64,128]{1,0:T(8,128)(2,1)} %param.20) | copy-start | bytes 49156
  153.7 39.3 %copy-start.16 = (bf16[256,64]{0,1:T(8,128)(2,1)S(1)}, bf16[256,64]{0,1:T(8,128)(2,1)}, u32[]{:S(2)}) copy-start(bf16[256,64]{0,1:T(8,128)(2,1)} %param.19) | copy-start | bytes 98308
  154.0 73.7 %copy-start.5 = (bf16[4,64,1,2048]{3,1,2,0:T(8,128)(2,1)S(1)}, bf16[4,64,1,2048]{3,1,2,0:T(8,128)(2,1)}, u32[]{:S(2)}) copy-start(bf16[4,64,1,2048]{3,1,2,0:T(8,128)(2,1)} %param.12) | copy-start | bytes 3145732
  227.7 0.6 copy-start.14
  231.0 2.0 copy-start
  233.0 4.2 copy-start.10
  233.9 6.6 copy-start.18
  238.6 5.6 copy-start.4
  240.5 1.9 copy-start.1
  243.3 0.8 copy-start.19
  244.1 3.1 copy-start.9
  244.1 3.1 copy-start.11
  250.5 1.9 copy-start.2
  253.4 0.8 copy-start.21
  254.2 3.1 copy-start.8
  254.2 3.1 copy-start.12
  260.5 1.9 copy-start.3
  263.6 0.8 copy-start.23
  264.4 3.1 copy-start.7
  264.4 3.1 copy-start.13
  269.0 4.8 copy-start.20
  269.0 4.8 copy-start.25
  273.8 4.8 copy-start.22
  273.8 4.8 copy-start.26
  278.6 4.8 copy-start.24
  278.6 4.8 copy-start.27
  288.3 3.7 copy-start.15
  288.3 3.7 copy-start.28
  288.3 3.7 copy-start.29
  288.3 3.7 copy-start.30
  294.1 434.0 %all-reduce.7.cloned.1.call-start = ((), (), s32[]{:S(2)}) async-start(), calls=%async_computation.3 | async-start | bytes 3145728 | tf_op jit(solution)/shard_map/psum | solution.py:16
Sparse Core Ops, SparseCore 0:
  10.1 77.2 all-gather.3
  89.5 70.0 all-gather.5
  294.3 272.7 all-reduce.4
  570.2 157.9 all-reduce.6
